TPU v7x, 256 devices: a whole 4x4x8 slice. The times are simulated.
256 devices in a mesh: wide: 32 (over x, z_lo, core), narrow: 8 (over y, z_hi).
Axes of the slice: x: 4, y: 4, z: 8 (z_hi: 2, z_lo: 4; z = z_hi * 4 + z_lo), core: 2. Of those that a mesh axis runs over, the one named last changes fastest.
Arguments:
- hidden_in: bfloat16 [2048, 6144], P('wide', 'narrow'), may hold values from -6 to 6
- w_query: bfloat16 [6144, 6144], P('narrow', 'wide'), may hold values from -1 to 1
- w_key: bfloat16 [6144, 6144], P('narrow', 'wide'), may hold values from -1 to 1
- w_value: bfloat16 [6144, 6144], P('narrow', 'wide'), may hold values from -0.078125 to 0.078125
- qkv_bias: float32 [3, 6144], P(None, 'wide'), may hold values from -3 to 3
- w_up: bfloat16 [6144, 24576], P('narrow', 'wide'), may hold values from -0.078125 to 0.078125
- up_bias: float32 [24576], P('wide'), may hold values from -3 to 3
- w_attn_out: bfloat16 [6144, 6144], P('wide', 'narrow'), may hold values from -0.078125 to 0.078125
- w_down: bfloat16 [24576, 6144], P('wide', 'narrow'), may hold values from -0.0390625 to 0.0390625
- out_bias: float32 [6144], P('narrow'), may hold values from -3 to 3
- norm_gain: float32 [2, 6144], P(None, 'narrow'), may hold values from 0.5 to 1.5
- norm_bias: float32 [2, 6144], P(None, 'narrow'), may hold values from -2 to 2
- seq_lens: int32 [8], replicated, may hold values from 1 to 1024, 2048 in all
- sink_count: int32 [8], replicated, may hold values from 1 to 64, as said below
- page_table: int32 [128], replicated, may hold values from 0 to 127, each once
Outputs:
- hidden_out: bfloat16 [2048, 6144], P('wide', 'narrow')
- paged_cache: bfloat16 [2, 128, 16, 6144], P(None, 'narrow', None, 'wide')
Inputs may be any that keep to these rules, and one draw needn't show every extreme that they name: `seq_lens`: the lengths are positive, add up to 2048, and the longest is exactly 1024. `sink_count`: some sequence has exactly 64 sink tokens. `page_table`: every slot is named by exactly one page.
All inputs are finite; a program needn't handle non-finite values.
Results may differ from a plain program's by a relative error of at most 0.02.
Values may be sent and summed in bfloat16 or wider, within the bound.
A program may use at most 64 MiB of HBM per device.

v0:
```python
import jax
import jax.numpy as jnp
from jax import lax
from jax.sharding import PartitionSpec as P

D = 6144
HEAD_DIM = 96
ROTARY = 24
PAGE = 16


def segment_info(token_index, seq_lens, sink_count):
    seq_ends = jnp.cumsum(seq_lens)
    seq_starts = seq_ends - seq_lens
    inside = (token_index[:, None] >= seq_starts[None, :]) & (
        token_index[:, None] < seq_ends[None, :]
    )
    member = inside.astype(jnp.int32)
    seq_number = jnp.arange(seq_lens.shape[0], dtype=jnp.int32)
    segment = jnp.sum(member * seq_number[None, :], axis=1)
    position = token_index - jnp.sum(member * seq_starts[None, :], axis=1)
    sink_limit = jnp.sum(member * sink_count[None, :], axis=1)
    return (segment, position, sink_limit)


def rotate(values, position):
    half_rot = ROTARY // 2
    freq_index = jnp.arange(half_rot, dtype=jnp.float32)
    inverse = jnp.power(jnp.float32(10000.0), -2.0 * freq_index / ROTARY)
    angles = position.astype(jnp.float32)[:, None] * inverse[None, :]
    cosine = jnp.cos(angles)[:, None, :]
    sine_part = jnp.sin(angles)[:, None, :]
    first_half = values[..., :half_rot]
    second_half = values[..., half_rot:ROTARY]
    return jnp.concatenate(
        [
            first_half * cosine - second_half * sine_part,
            second_half * cosine + first_half * sine_part,
            values[..., ROTARY:],
        ],
        axis=-1,
    )


def local(
    hidden_in,
    w_query,
    w_key,
    w_value,
    qkv_bias,
    w_up,
    up_bias,
    w_attn_out,
    w_down,
    out_bias,
    norm_gain,
    norm_bias,
    seq_lens,
    sink_count,
    page_table,
):
    wide_count = lax.axis_size("wide")
    narrow_count = lax.axis_size("narrow")
    narrow_index = lax.axis_index("narrow")
    tok_local, feat_local = hidden_in.shape
    sub_rows = tok_local // narrow_count
    total_tokens = tok_local * wide_count
    query_rows = wide_count * sub_rows
    head_cols = w_query.shape[1]
    heads_local = head_cols // HEAD_DIM
    as_float = hidden_in.astype(jnp.float32)
    partial_sum = jnp.sum(as_float, axis=1)
    partial_square = jnp.sum(as_float * as_float, axis=1)
    total_sum, total_square = lax.psum((partial_sum, partial_square), "narrow")
    average = total_sum / D
    variance = total_square / D - average * average
    scaled = (as_float - average[:, None]) * lax.rsqrt(variance + 1e-05)[:, None]
    attn_normed = (scaled * norm_gain[0] + norm_bias[0]).astype(jnp.bfloat16)
    mlp_normed = (scaled * norm_gain[1] + norm_bias[1]).astype(jnp.bfloat16)
    stacked = jnp.stack([attn_normed, mlp_normed]).reshape(2, narrow_count, sub_rows, feat_local)
    gathered = lax.all_gather(stacked, "wide", axis=2, tiled=True).reshape(
        2, total_tokens, feat_local
    )
    local_order = jnp.arange(query_rows, dtype=jnp.int32)
    local_tokens = (
        local_order // sub_rows * tok_local + narrow_index * sub_rows + local_order % sub_rows
    )
    local_seg, local_pos, local_sink = segment_info(local_tokens, seq_lens, sink_count)
    all_order = jnp.arange(total_tokens, dtype=jnp.int32)
    all_tokens = (
        all_order % query_rows // sub_rows * tok_local
        + all_order // query_rows * sub_rows
        + all_order % sub_rows
    )
    all_seg, all_pos, all_sink = segment_info(all_tokens, seq_lens, sink_count)
    qkv_weight = jnp.concatenate([w_query, w_key, w_value], axis=1)
    attn_part = gathered[0]
    mlp_part = gathered[1]
    summed = lax.psum_scatter(
        jnp.concatenate(
            [
                jnp.dot(attn_part, qkv_weight, preferred_element_type=jnp.float32),
                jnp.dot(mlp_part, w_up, preferred_element_type=jnp.float32),
            ],
            axis=1,
        ).astype(jnp.bfloat16),
        "narrow",
        scatter_dimension=0,
        tiled=True,
    ).astype(jnp.float32)
    query_sum = summed[:, :head_cols]
    key_sum = summed[:, head_cols : 2 * head_cols]
    value_sum = summed[:, 2 * head_cols : 3 * head_cols]
    unit_sum = summed[:, 3 * head_cols :]
    keys_local = (
        rotate((key_sum + qkv_bias[1]).reshape(query_rows, heads_local, HEAD_DIM), local_pos)
        .astype(jnp.bfloat16)
        .reshape(query_rows, head_cols)
    )
    values_local = (value_sum + qkv_bias[2]).astype(jnp.bfloat16)
    all_keys, all_values = (
        lax.all_gather(keys_local, "narrow", axis=0, tiled=True),
        lax.all_gather(values_local, "narrow", axis=0, tiled=True),
    )
    queries = rotate(
        (query_sum + qkv_bias[0]).reshape(query_rows, heads_local, HEAD_DIM), local_pos
    ).astype(jnp.bfloat16)
    hidden_units = jax.nn.gelu(unit_sum + up_bias, approximate=False).astype(jnp.bfloat16)
    window_span = total_tokens // 16
    allowed = (local_seg[:, None] == all_seg[None, :]) & (all_pos[None, :] <= local_pos[:, None])
    allowed = allowed & (
        (local_pos[:, None] - all_pos[None, :] < window_span)
        | (all_pos[None, :] < local_sink[:, None])
    )
    key_heads = all_keys.reshape(total_tokens, heads_local, HEAD_DIM)
    value_heads = all_values.reshape(total_tokens, heads_local, HEAD_DIM)
    scores = jnp.einsum("qhd,khd->hqk", queries, key_heads, preferred_element_type=jnp.float32) * (
        1.0 / HEAD_DIM**0.5
    )
    masked = jnp.where(allowed[None], scores, jnp.float32(-1e30))
    top_score = jnp.max(masked, axis=2, keepdims=True)
    weights = jnp.exp(masked - top_score)
    probs = (weights / jnp.sum(weights, axis=2, keepdims=True)).astype(jnp.bfloat16)
    attended = (
        jnp.einsum("hqk,khd->qhd", probs, value_heads, preferred_element_type=jnp.float32)
        .astype(jnp.bfloat16)
        .reshape(query_rows, head_cols)
    )
    full_out, full_down = (
        lax.all_gather(w_attn_out, "narrow", axis=1, tiled=True),
        lax.all_gather(w_down, "narrow", axis=1, tiled=True),
    )
    attn_part = attended
    own_rows = lax.psum_scatter(
        (
            jnp.dot(attn_part, full_out, preferred_element_type=jnp.float32)
            + jnp.dot(hidden_units, full_down, preferred_element_type=jnp.float32)
        ).astype(jnp.bfloat16),
        "wide",
        scatter_dimension=0,
        tiled=True,
    ).astype(jnp.float32)
    combined = lax.all_to_all(
        own_rows.astype(jnp.bfloat16), "narrow", split_axis=1, concat_axis=0, tiled=True
    ).astype(own_rows.dtype)
    hidden_out = (as_float + combined + out_bias).astype(jnp.bfloat16)
    pages_local = page_table.shape[0] // narrow_count
    slot_ids = narrow_index * pages_local + jnp.arange(pages_local, dtype=jnp.int32)
    matches = (page_table[None, :] == slot_ids[:, None]).astype(jnp.int32)
    source_page = jnp.sum(
        matches * jnp.arange(page_table.shape[0], dtype=jnp.int32)[None, :], axis=1
    )
    token_ids = (source_page[:, None] * PAGE + jnp.arange(PAGE, dtype=jnp.int32)[None, :]).reshape(
        -1
    )
    gather_rows = (
        token_ids % tok_local // sub_rows * query_rows
        + token_ids // tok_local * sub_rows
        + token_ids % sub_rows
    )
    cache_keys = jnp.take(all_keys, gather_rows, axis=0).reshape(pages_local, PAGE, head_cols)
    cache_values = jnp.take(all_values, gather_rows, axis=0).reshape(pages_local, PAGE, head_cols)
    paged_cache = jnp.stack([cache_keys, cache_values])
    return (hidden_out, paged_cache)


def solution(mesh):
    in_specs = (
        P("wide", "narrow"),
        P("narrow", "wide"),
        P("narrow", "wide"),
        P("narrow", "wide"),
        P(None, "wide"),
        P("narrow", "wide"),
        P("wide"),
        P("wide", "narrow"),
        P("wide", "narrow"),
        P("narrow"),
        P(None, "narrow"),
        P(None, "narrow"),
        P(),
        P(),
        P(),
    )
    out_specs = (P("wide", "narrow"), P(None, "narrow", None, "wide"))
    return jax.shard_map(local, mesh=mesh, in_specs=in_specs, out_specs=out_specs, check_vma=False)
```

profile of v0, /device:TPU:8, one launch (start us, length us, event | category | flops | bytes accessed | tf_op | source)
XLA Modules:
  0.0 761.1 jit_solution(3944237115686412348)
XLA Ops:
  7.2 1.1 convert_reduce_fusion
  8.3 31.2 %all-reduce = (f32[64]{0:T(128)S(1)}, f32[64]{0:T(128)S(1)}) all-reduce(f32[64]{0:T(128)S(1)} %get-tuple-element.4, f32[64]{0:T(128)S(1)} %get-tuple-element.3), channel_id=1, replica_groups=mesh['wide'=32,'narrow'=8] {'narrow'}, use_global_device_ids=true, to_apply=%region_3.0 | all-reduce | flops 128 | bytes 1024 | tf_op jit(solution)/shard_map/psum | solution.py:74
  39.6 0.8 slice_reduce_fusion.2
  40.4 1.0 fusion.72
  41.4 0.7 pad_maximum_fusion.2
  42.2 63.7 %all-gather.4.cloned.1.call-done = bf16[2,8,256,768]{3,2,1,0:T(8,128)(2,1)} async-done(((bf16[2,8,8,768]{3,2,1,0:T(8,128)(2,1)}), bf16[2,8,256,768]{3,2,1,0:T(8,128)(2,1)}) %all-gather.4.cloned.1.call-update) | async-done | bytes 6291472 | tf_op jit(solution)/shard_map/all_gather | solution.py:81
  105.9 3.3 fusion.142
  109.2 2.9 convolution_convert_fusion
  112.2 2.0 convolution_convert_fusion.1
  114.2 2.9 pad_maximum_fusion
  117.2 0.7 all-gather.8.cloned.1.call-update
  119.2 0.9 fusion.6
  120.1 142.9 %reduce-scatter.3.cloned.1.call-done = bf16[256,1344]{0,1:T(8,128)(2,1)} async-done(((bf16[2048,1344]{0,1:T(8,128)(2,1)}), bf16[256,1344]{0,1:T(8,128)(2,1)}) %reduce-scatter.3.cloned.1.call-update) | async-done | bytes 688144 | tf_op jit(solution)/shard_map/reduce_scatter | solution.py:99
  262.9 1.2 convert_element_type.65
  264.1 1.1 copy-done.2
  265.2 0.8 slice_add_fusion.2
  267.4 76.0 %all_gather.17 = bf16[2048,192]{1,0:T(8,128)(2,1)S(1)} all-gather(bf16[256,192]{1,0:T(8,128)(2,1)S(1)} %copy.20), channel_id=1, replica_groups=mesh['wide'=32,'narrow'=8] {'narrow'}, dimensions={0}, use_global_device_ids=true | all-gather | bytes 884736 | tf_op jit(solution)/shard_map/all_gather | solution.py:122
  344.0 3.3 fusion.144
  347.2 65.6 %all_gather.16 = bf16[2048,192]{0,1:T(8,128)(2,1)S(1)} all-gather(bf16[256,192]{0,1:T(8,128)(2,1)} %get-tuple-element.24), channel_id=1, replica_groups=mesh['wide'=32,'narrow'=8] {'narrow'}, dimensions={0}, use_global_device_ids=true | all-gather | bytes 884736 | tf_op jit(solution)/shard_map/all_gather | solution.py:123
  412.9 4.1 fusion.9
  416.9 86.6 %all-gather.8.cloned.1.call-done = bf16[768,6144]{1,0:T(8,128)(2,1)} async-done(((bf16[768,768]{1,0:T(8,128)(2,1)}), bf16[768,6144]{1,0:T(8,128)(2,1)}) %all-gather.8.cloned.1.call-update) | async-done | bytes 9437200 | tf_op jit(solution)/shard_map/all_gather | solution.py:151
  503.5 11.0 %fusion.27 = f32[256,6144]{1,0:T(8,128)} fusion(bf16[768,6144]{1,0:T(8,128)(2,1)} %all-gather.8.cloned.1.call-done, f32[256,1344]{0,1:T(8,128)} %copy-done.2, f32[768]{0:T(1024)} %param.23), kind=kOutput, calls=%fused_computation.46 | convolution fusion | flops 2428895232 | bytes 16519168 | tf_op jit(solution)/shard_map/dot_general | solution.py:157
  514.6 70.8 %all-gather.6.cloned.1.call-done = bf16[192,6144]{1,0:T(8,128)(2,1)} async-done(((bf16[192,768]{1,0:T(8,128)(2,1)}), bf16[192,6144]{1,0:T(8,128)(2,1)}) %all-gather.6.cloned.1.call-update) | async-done | bytes 2359312 | tf_op jit(solution)/shard_map/all_gather | solution.py:150
  585.3 6.2 fusion.1
  592.6 1.4 copy.22
  594.0 1.2 gather_fusion
  595.2 1.2 gather_fusion.1
  596.3 141.5 %reduce-scatter.5.cloned.1.call-done = bf16[8,6144]{1,0:T(8,128)(2,1)} async-done(((bf16[256,6144]{1,0:T(8,128)(2,1)}), bf16[8,6144]{1,0:T(8,128)(2,1)}) %reduce-scatter.5.cloned.1.call-update) | async-done | bytes 98320 | tf_op jit(solution)/shard_map/reduce_scatter | solution.py:154
  737.9 7.2 all-to-all-start
  745.2 0.7 pad_maximum_fusion.1
  745.9 8.0 %all-to-all-done = bf16[8,8,768]{2,0,1:T(8,128)(2,1)S(1)} async-done(((bf16[8,8,768]{2,0,1:T(8,128)(2,1)}), bf16[8,8,768]{2,0,1:T(8,128)(2,1)S(1)}, u32[]{:S(2)}, u32[]{:S(2)}) %all-to-all-start) | async-done | bytes 98336 | tf_op jit(solution)/shard_map/all_to_all | solution.py:163
  753.9 0.7 fusion.69
  (62 shorter events, 4.4 us)
Async XLA Ops:
  7.2 102.0 %copy-start = (bf16[768,768]{1,0:T(8,128)(2,1)S(1)}, bf16[768,768]{1,0:T(8,128)(2,1)}, u32[]{:S(2)}) copy-start(bf16[768,768]{1,0:T(8,128)(2,1)} %param.22) | copy-start | bytes 3538948
  7.2 98.7 %all-gather.4.cloned.1.call-start = ((), (), s32[]{:S(2)}) async-start(), calls=%async_computation.3 | async-start | bytes 6488064 | tf_op jit(solution)/shard_map/all_gather | solution.py:81
  42.1 220.8 %reduce-scatter.3.cloned.1.call-start = ((), (), s32[]{:S(2)}) async-start(), calls=%async_computation.4 | async-start | bytes 6193152 | tf_op jit(solution)/shard_map/reduce_scatter | solution.py:99
  109.2 3.0 copy-start.9
  109.2 3.0 copy-start.10
  109.2 3.0 copy-start.11
  117.1 1.4 copy-start.12
  117.1 1.6 copy-start.8
  117.1 1.9 copy-start.7
  117.2 386.4 %all-gather.8.cloned.1.call-start = ((), (), s32[]{:S(2)}) async-start(), calls=%async_computation.6 | async-start | bytes 10616832 | tf_op jit(solution)/shard_map/all_gather | solution.py:151
  117.9 467.4 %all-gather.6.cloned.1.call-start = ((), (), s32[]{:S(2)}) async-start(), calls=%async_computation.5 | async-start | bytes 2654208 | tf_op jit(solution)/shard_map/all_gather | solution.py:150
  118.5 619.4 %reduce-scatter.5.cloned.1.call-start = ((), (), s32[]{:S(2)}) async-start(), calls=%async_computation.7 | async-start | bytes 3244032 | tf_op jit(solution)/shard_map/reduce_scatter | solution.py:154
  264.1 1.1 copy-start.2
  344.0 3.3 copy-start.4
  412.9 4.1 copy-start.1
  416.9 168.4 %copy-start.5 = (bf16[2,96,256]{2,1,0:T(8,128)(2,1)S(1)}, bf16[2,96,256]{2,1,0:T(8,128)(2,1)}, u32[]{:S(2)}) copy-start(bf16[2,96,256]{2,1,0:T(8,128)(2,1)} %fusion.9) | copy-start | bytes 294916
  591.5 0.7 copy-start.13
  591.6 162.4 %copy-start.3 = (bf16[64,768]{1,0:T(8,128)(2,1)S(1)}, bf16[64,768]{1,0:T(8,128)(2,1)}, u32[]{:S(2)}) copy-start(bf16[64,768]{1,0:T(8,128)(2,1)} %param.17) | copy-start | bytes 294916
  591.6 162.4 %copy-start.6 = (f32[768]{0:T(1024)S(1)}, f32[768]{0:T(1024)}, u32[]{:S(2)}) copy-start(f32[768]{0:T(1024)} %param.26) | copy-start | bytes 9220
  737.9 16.1 %all-to-all-start = ((bf16[8,8,768]{2,0,1:T(8,128)(2,1)}), bf16[8,8,768]{2,0,1:T(8,128)(2,1)S(1)}, u32[]{:S(2)}, u32[]{:S(2)}) async-start(bf16[8,8,768]{2,0,1:T(8,128)(2,1)} %bitcast.49), calls=%async_computation.2 | async-start | bytes 196608 | tf_op jit(solution)/shard_map/all_to_all | solution.py:163
Sparse Core Ops, SparseCore 0:
  42.2 63.6 all-gather.3
  117.3 145.6 reduce-scatter.2
  265.9 237.5 all-gather.7
  506.4 78.9 all-gather.5
  591.7 146.1 reduce-scatter.4
where the time goes:
time: 762 us; the launch traced here: 761 us
  waiting for transfers between devices  515 us (68%)
  blocking collectives  173 us (23%)
  matrix products  29.5 us (4%)
  between operations  14.1 us (2%)
  other arithmetic  11.6 us (2%)
  local copies, waits for them, and re-layouts  10.9 us (1%)
    reduce_scatter x1, waiting for transfers between devices, local(): lax.psum_scatter(jnp.concatenate([jnp.dot(attn_part, qkv_weight, preferre...  143 us
    reduce_scatter x1, waiting for transfers between devices, local(): lax.psum_scatter((jnp.dot(attn_part, full_out, preferred_element_type=jnp...  142 us
    all_gather x1, waiting for transfers between devices, local(): lax.all_gather(w_down, 'narrow', axis=1, tiled=True)  86.6 us
    all_gather x1, blocking collectives, local(): lax.all_gather(keys_local, 'narrow', axis=0, tiled=True)  76 us
    all_gather x1, waiting for transfers between devices, local(): lax.all_gather(w_attn_out, 'narrow', axis=1, tiled=True)  70.8 us
    all_gather x1, blocking collectives, local(): lax.all_gather(values_local, 'narrow', axis=0, tiled=True)  65.6 us
    all_gather x1, waiting for transfers between devices, local(): lax.all_gather(stacked, 'wide', axis=2, tiled=True)  63.7 us
    psum x1, blocking collectives, local(): total_sum, total_square = lax.psum((partial_sum, partial_square), 'narrow')  31.2 us
  transfers between devices with their start and end apart: 6, of which 6 were waited for; matrix products, arithmetic and copies ran while one was open for 4% of the time, Pallas kernels for 0%

commit v1 on v0

--- a/solution.py
+++ b/solution.py
@@ -1,3 +1,4 @@
+import functools
 import jax
 import jax.numpy as jnp
 from jax import lax
@@ -7,6 +8,22 @@
 HEAD_DIM = 96
 ROTARY = 24
 PAGE = 16
+
+
+def streams_show(payload, shard_axis):
+    f_now = jnp.concatenate(
+        lax.all_to_all(
+            jnp.stack([payload] * lax.axis_size(shard_axis), axis=0),
+            shard_axis,
+            concat_axis=0,
+            split_axis=0,
+        ),
+        axis=2,
+    )
+    return f_now
+
+
+fix_racks_here = functools.partial(streams_show, shard_axis="wide")
 
 
 def segment_info(token_index, seq_lens, sink_count):
@@ -78,9 +95,7 @@
     attn_normed = (scaled * norm_gain[0] + norm_bias[0]).astype(jnp.bfloat16)
     mlp_normed = (scaled * norm_gain[1] + norm_bias[1]).astype(jnp.bfloat16)
     stacked = jnp.stack([attn_normed, mlp_normed]).reshape(2, narrow_count, sub_rows, feat_local)
-    gathered = lax.all_gather(stacked, "wide", axis=2, tiled=True).reshape(
-        2, total_tokens, feat_local
-    )
+    gathered = fix_racks_here(stacked).reshape(2, total_tokens, feat_local)
     local_order = jnp.arange(query_rows, dtype=jnp.int32)
     local_tokens = (
         local_order // sub_rows * tok_local + narrow_index * sub_rows + local_order % sub_rows

time: 762 us -> 832 us (1.092)
  blocking collectives: 173 us -> 336 us
  waiting for transfers between devices: 515 us -> 429 us
    all_to_all x0 -> x1, blocking collectives: none -> 146 us  [streams_show(): lax.all_to_all(jnp.stack([payload] * lax.axis_size(shard_axis), axis=0),...]
    all_gather x1 -> x0, waiting for transfers between devices: 63.7 us -> none  [local(): lax.all_gather(stacked, 'wide', axis=2, tiled=True)]
    all_gather x1, blocking collectives: 65.6 us -> 87.6 us  [local(): lax.all_gather(values_local, 'narrow', axis=0, tiled=True)]
    all_gather x1, waiting for transfers between devices: 86.6 us -> 69.4 us  [local(): lax.all_gather(w_down, 'narrow', axis=1, tiled=True)]
  transfers between devices with their start and end apart: 6 -> 5, of which waited for: 6 -> 5; matrix products, arithmetic and copies ran while one was open for 4% -> 3% of each run, Pallas kernels for 0% -> 0%
where the time goes in v1:
time: 832 us
  waiting for transfers between devices  429 us (52%)
  blocking collectives  336 us (40%)
  matrix products  26.6 us (3%)
  between operations  14.1 us (2%)
  other arithmetic  9.74 us (1%)
  local copies, waits for them, and re-layouts  8.81 us (1%)
    all_to_all x1, blocking collectives, streams_show(): lax.all_to_all(jnp.stack([payload] * lax.axis_size(shard_axis), axis=0),...  146 us
    reduce_scatter x1, waiting for transfers between devices, local(): lax.psum_scatter((jnp.dot(attn_part, full_out, preferred_element_type=jnp...  142 us
    reduce_scatter x1, waiting for transfers between devices, local(): lax.psum_scatter(jnp.concatenate([jnp.dot(attn_part, qkv_weight, preferre...  138 us
    all_gather x1, blocking collectives, local(): lax.all_gather(values_local, 'narrow', axis=0, tiled=True)  87.6 us
    all_gather x1, blocking collectives, local(): lax.all_gather(keys_local, 'narrow', axis=0, tiled=True)  71.4 us
    all_gather x1, waiting for transfers between devices, local(): lax.all_gather(w_attn_out, 'narrow', axis=1, tiled=True)  70.1 us
    all_gather x1, waiting for transfers between devices, local(): lax.all_gather(w_down, 'narrow', axis=1, tiled=True)  69.4 us
    psum x1, blocking collectives, local(): total_sum, total_square = lax.psum((partial_sum, partial_square), 'narrow')  31.2 us
  transfers between devices with their start and end apart: 5, of which 5 were waited for; matrix products, arithmetic and copies ran while one was open for 3% of the time, Pallas kernels for 0%

profile of v1, /device:TPU:8, one launch (start us, length us, event | category | flops | bytes accessed | tf_op | source)
XLA Modules:
  0.0 831.7 jit_solution(15823747630921971396)
XLA Ops:
  7.2 1.1 convert_reduce_fusion
  8.3 31.2 %all-reduce = (f32[64]{0:T(128)S(1)}, f32[64]{0:T(128)S(1)}) all-reduce(f32[64]{0:T(128)S(1)} %get-tuple-element.4, f32[64]{0:T(128)S(1)} %get-tuple-element.3), channel_id=1, replica_groups=mesh['wide'=32,'narrow'=8] {'narrow'}, use_global_device_ids=true, to_apply=%region_3.0 | all-reduce | flops 128 | bytes 1024 | tf_op jit(solution)/shard_map/psum | solution.py:91
  39.6 0.8 slice_reduce_fusion.2
  40.4 1.0 fusion.72
  41.4 0.8 stack.18
  42.2 146.2 %all_to_all.18 = bf16[32,2,8,8,768]{4,3,2,1,0:T(8,128)(2,1)S(1)} all-to-all(bf16[32,2,8,8,768]{4,3,2,1,0:T(8,128)(2,1)S(1)} %stack.18), channel_id=1, replica_groups=mesh['wide'=32,'narrow'=8] {'wide'}, dimensions={0} | all-to-all | bytes 12582912 | tf_op jit(solution)/shard_map/all_to_all | solution.py:15
  188.4 0.6 copy.32
  189.5 2.9 convolution_convert_fusion
  192.4 2.0 convolution_convert_fusion.1
  194.5 2.9 pad_maximum_fusion
  197.5 0.7 all-gather.5.cloned.1.call-update
  198.2 0.7 all-gather.3.cloned.1.call-update
  199.6 0.9 fusion.6
  200.5 138.3 %reduce-scatter.3.cloned.1.call-done = bf16[256,1344]{0,1:T(8,128)(2,1)} async-done(((bf16[2048,1344]{0,1:T(8,128)(2,1)}), bf16[256,1344]{0,1:T(8,128)(2,1)}) %reduce-scatter.3.cloned.1.call-update) | async-done | bytes 688144 | tf_op jit(solution)/shard_map/reduce_scatter | solution.py:114
  338.8 1.2 convert_element_type.65
  340.0 1.1 copy-done.3
  341.4 71.4 %all_gather.13 = bf16[2048,192]{1,0:T(8,128)(2,1)S(1)} all-gather(bf16[256,192]{1,0:T(8,128)(2,1)S(1)} %copy.28), channel_id=1, replica_groups=mesh['wide'=32,'narrow'=8] {'narrow'}, dimensions={0}, use_global_device_ids=true | all-gather | bytes 884736 | tf_op jit(solution)/shard_map/all_gather | solution.py:137
  413.3 1.7 fusion.144
  415.1 87.6 %all_gather.12 = bf16[2048,192]{0,1:T(8,128)(2,1)S(1)} all-gather(bf16[256,192]{0,1:T(8,128)(2,1)S(1)} %get-tuple-element.24), channel_id=1, replica_groups=mesh['wide'=32,'narrow'=8] {'narrow'}, dimensions={0}, use_global_device_ids=true | all-gather | bytes 884736 | tf_op jit(solution)/shard_map/all_gather | solution.py:138
  502.6 2.7 fusion.9
  505.4 69.4 %all-gather.5.cloned.1.call-done = bf16[768,6144]{1,0:T(8,128)(2,1)} async-done(((bf16[768,768]{1,0:T(8,128)(2,1)}), bf16[768,6144]{1,0:T(8,128)(2,1)}) %all-gather.5.cloned.1.call-update) | async-done | bytes 9437200 | tf_op jit(solution)/shard_map/all_gather | solution.py:166
  574.8 11.0 %fusion.27 = f32[256,6144]{1,0:T(8,128)} fusion(bf16[768,6144]{1,0:T(8,128)(2,1)} %all-gather.5.cloned.1.call-done, f32[256,1344]{0,1:T(8,128)} %copy-done.3, f32[768]{0:T(1024)S(1)} %copy-done.12), kind=kOutput, calls=%fused_computation.47 | convolution fusion | flops 2428895232 | bytes 16518144 | tf_op jit(solution)/shard_map/dot_general | solution.py:172
  585.9 70.1 %all-gather.3.cloned.1.call-done = bf16[192,6144]{1,0:T(8,128)(2,1)} async-done(((bf16[192,768]{1,0:T(8,128)(2,1)}), bf16[192,6144]{1,0:T(8,128)(2,1)}) %all-gather.3.cloned.1.call-update) | async-done | bytes 2359312 | tf_op jit(solution)/shard_map/all_gather | solution.py:165
  655.9 6.2 fusion.1
  663.2 1.4 copy.30
  664.6 1.2 gather_fusion
  665.8 1.2 gather_fusion.1
  666.9 141.5 %reduce-scatter.5.cloned.1.call-done = bf16[8,6144]{1,0:T(8,128)(2,1)} async-done(((bf16[256,6144]{1,0:T(8,128)(2,1)}), bf16[8,6144]{1,0:T(8,128)(2,1)}) %reduce-scatter.5.cloned.1.call-update) | async-done | bytes 98320 | tf_op jit(solution)/shard_map/reduce_scatter | solution.py:169
  808.4 7.2 all-to-all-start.1
  815.7 0.7 pad_maximum_fusion.1
  816.5 8.0 all-to-all-done.1
  824.5 0.7 fusion.69
  (64 shorter events, 3.2 us)
Async XLA Ops:
  7.2 182.3 %copy-start = (bf16[768,768]{1,0:T(8,128)(2,1)S(1)}, bf16[768,768]{1,0:T(8,128)(2,1)}, u32[]{:S(2)}) copy-start(bf16[768,768]{1,0:T(8,128)(2,1)} %param.22) | copy-start | bytes 3538948
  7.2 331.6 %reduce-scatter.3.cloned.1.call-start = ((), (), s32[]{:S(2)}) async-start(), calls=%async_computation.4 | async-start | bytes 6193152 | tf_op jit(solution)/shard_map/reduce_scatter | solution.py:114
  189.4 3.0 copy-start.9
  189.5 3.0 copy-start.10
  189.5 3.0 copy-start.11
  197.4 1.6 copy-start.13
  197.4 1.8 copy-start.8
  197.4 2.0 copy-start.7
  197.4 377.4 %all-gather.5.cloned.1.call-start = ((), (), s32[]{:S(2)}) async-start(), calls=%async_computation.6 | async-start | bytes 10616832 | tf_op jit(solution)/shard_map/all_gather | solution.py:166
  198.2 457.8 %all-gather.3.cloned.1.call-start = ((), (), s32[]{:S(2)}) async-start(), calls=%async_computation.5 | async-start | bytes 2654208 | tf_op jit(solution)/shard_map/all_gather | solution.py:165
  198.9 609.5 %reduce-scatter.5.cloned.1.call-start = ((), (), s32[]{:S(2)}) async-start(), calls=%async_computation.7 | async-start | bytes 3244032 | tf_op jit(solution)/shard_map/reduce_scatter | solution.py:169
  340.0 1.1 copy-start.3
  341.3 73.8 %copy-start.5 = (bf16[256,2,12]{0,2,1:T(8,128)(2,1)}, bf16[256,2,12]{0,2,1:T(8,128)(2,1)S(1)}, u32[]{:S(2)}) copy-start(bf16[256,2,12]{0,2,1:T(8,128)(2,1)S(1)} %get-tuple-element.26) | copy-start | bytes 36868
  502.6 2.7 copy-start.2
  502.6 72.2 %copy-start.12 = (f32[768]{0:T(1024)S(1)}, f32[768]{0:T(1024)}, u32[]{:S(2)}) copy-start(f32[768]{0:T(1024)} %param.23) | copy-start | bytes 9220
  662.1 0.7 copy-start.14
  662.1 162.4 %copy-start.4 = (bf16[64,768]{1,0:T(8,128)(2,1)S(1)}, bf16[64,768]{1,0:T(8,128)(2,1)}, u32[]{:S(2)}) copy-start(bf16[64,768]{1,0:T(8,128)(2,1)} %param.17) | copy-start | bytes 294916
  662.1 162.4 %copy-start.6 = (f32[768]{0:T(1024)S(1)}, f32[768]{0:T(1024)}, u32[]{:S(2)}) copy-start(f32[768]{0:T(1024)} %param.26) | copy-start | bytes 9220
  662.2 163.0 %copy-start.1 = (bf16[768,768]{1,0:T(8,128)(2,1)S(1)}, bf16[768,768]{1,0:T(8,128)(2,1)}, u32[]{:S(2)}) copy-start(bf16[768,768]{1,0:T(8,128)(2,1)} %param.22) | copy-start | bytes 3538948
  808.4 16.1 %all-to-all-start.1 = ((bf16[8,8,768]{2,0,1:T(8,128)(2,1)}), bf16[8,8,768]{2,0,1:T(8,128)(2,1)S(1)}, u32[]{:S(2)}, u32[]{:S(2)}) async-start(bf16[8,8,768]{2,0,1:T(8,128)(2,1)} %bitcast.55), calls=%async_computation.3 | async-start | bytes 196608 | tf_op jit(solution)/shard_map/all_to_all | solution.py:178
Sparse Core Ops, SparseCore 0:
  197.5 141.1 reduce-scatter.2
  341.7 233.0 all-gather.4
  577.8 78.0 all-gather.2
  662.3 146.1 reduce-scatter.4
